TPU v7x, 32 devices: a whole 2x2x4 slice. The times are simulated.
32 devices in a mesh: groups: 2 (over x), ctx: 4 (over y, core), heads: 4 (over z).
Axes of the slice: x: 2, y: 2, z: 4, core: 2. Of those that a mesh axis runs over, the one named last changes fastest.
Arguments:
- tokens: bfloat16 [4096, 2048], P(('groups', 'ctx', 'heads')), parts along dimension 0, may hold values from -60 to 60
- state_in: float32 [4, 256, 128], P('heads', 'groups'), parts along dimension 1, may hold values from -256 to 256
- past_kv: bfloat16 [2, 1024, 512], P(None, 'groups', 'heads'), parts along dimension 1, may hold values from -6 to 6
- w_qkv: bfloat16 [2048, 3, 512], P(None, None, 'heads'), may hold values from -0.125 to 0.125
- w_out: bfloat16 [512, 2048], P('heads'), may hold values from -0.25 to 0.25
- w_gate: bfloat16 [16, 2048, 768], P(('ctx', 'heads')), may hold values from -0.125 to 0.125
- w_up: bfloat16 [16, 2048, 768], P(('ctx', 'heads')), may hold values from -0.125 to 0.125
- w_down: bfloat16 [16, 768, 2048], P(('ctx', 'heads')), may hold values from -0.21875 to 0.21875
- expert_ids: int32 [4096, 8], P(('groups', 'ctx', 'heads')), parts along dimension 0, may hold values from 0 to 15, all different within a row; in each aligned block of 128 rows (0 to 127, 128 to 255, ...) at most 128 rows name the same one
- gate_weights: float32 [4096, 8], P(('groups', 'ctx', 'heads')), parts along dimension 0, may hold values from 0.1 to 1
Outputs:
- mixed: bfloat16 [4096, 2048], P(('groups', 'ctx', 'heads')), parts along dimension 0
There are 2 independent parts, one for each index of `groups`. A program takes and returns all parts, laid end to end along the dimension named above; an argument that names none is the same for every part. Nothing has to cross between parts.
Inputs may be any that keep to these rules, and one draw needn't show every extreme that they name: `expert_ids`: each row names 8 different experts; in each aligned block of 128 rows (the rows of one device) no expert is named by more than 128 rows, a bound that some block reaches.
All inputs are finite; a program needn't handle non-finite values.
Results may differ from a plain program's by a relative error of at most 0.017.
Values may be sent and summed in bfloat16 or wider, within the bound.
A program may use at most 128 MiB of HBM per device.

v0:
```python
import math
import jax
import jax.numpy as jnp
from jax import lax
from jax.sharding import PartitionSpec as P

HDIM = 128
WINDOW = 512


def entering(x, axis, join, neutral):
    place = lax.axis_index(axis)
    gathered = lax.all_gather(x.astype(jnp.bfloat16), axis)
    state = jnp.zeros_like(x) + jnp.asarray(neutral, x.dtype)

    def one(lap, state):
        return join(state, lax.dynamic_index_in_dim(gathered, lap, 0, False).astype(x.dtype))

    return lax.fori_loop(0, place, one, state)


def from_behind(block, axis, distance):
    devices = range(lax.axis_size(axis))
    route = [(i - distance, i) for i in devices if i - distance in devices]
    return lax.ppermute(block, axis, route)


def normalize(value):
    return value * lax.rsqrt(jnp.mean(value * value, axis=-1, keepdims=True) + 1e-06)


def dense_experts(
    hidden_float, normed, w_gate, w_up, w_down, expert_ids, gate_weights, expert_count
):
    axes = ("ctx", "heads")
    exp_local = w_gate.shape[0]
    chosen = expert_ids[:, :, None] == jnp.arange(expert_count, dtype=jnp.int32)
    table = jnp.sum(jnp.where(chosen, gate_weights[:, :, None], 0.0), axis=1)
    weights = lax.all_gather(table, axes, axis=0, tiled=True)
    first = lax.axis_index(axes) * exp_local
    rows = lax.all_gather(normed, axes, axis=0, tiled=True)
    total = None
    for e in range(exp_local):
        gate_act = jnp.dot(rows, w_gate[e], preferred_element_type=jnp.float32)
        up_act = jnp.dot(rows, w_up[e], preferred_element_type=jnp.float32)
        hid = (jax.nn.silu(gate_act) * up_act).astype(jnp.bfloat16)
        out_rows = jnp.dot(hid, w_down[e], preferred_element_type=jnp.float32)
        weight = lax.dynamic_slice_in_dim(weights, first + e, 1, 1)
        part = weight * out_rows
        total = part if total is None else total + part
    routed = lax.psum_scatter(total.astype(jnp.bfloat16), axes, scatter_dimension=0, tiled=True)
    return (hidden_float + routed.astype(jnp.float32)).astype(jnp.bfloat16)


def on_device(
    tokens, state_in, past_kv, w_qkv, w_out, w_gate, w_up, w_down, expert_ids, gate_weights
):
    row_count, model_width = tokens.shape
    inner_width = w_qkv.shape[2]
    local_heads = inner_width // HDIM
    w_flat = w_qkv.reshape(model_width, 3 * inner_width)
    projected = jnp.dot(
        lax.all_gather(tokens, "heads", axis=0, tiled=True),
        w_flat,
        preferred_element_type=jnp.float32,
    ).astype(jnp.bfloat16)
    slab_rows = projected.shape[0]
    projected = projected.reshape(slab_rows, 3, local_heads, HDIM)
    query = jnp.transpose(projected[:, 0], (1, 0, 2))
    keys = jnp.transpose(projected[:, 1], (1, 0, 2))
    values = jnp.transpose(projected[:, 2], (1, 0, 2))
    local_state = jnp.einsum("hsd,hse->hde", keys, values, preferred_element_type=jnp.float32)
    earlier_state = entering(
        local_state, "ctx", lambda first, second: first + second, jnp.zeros_like(local_state)
    )
    start_state = state_in + earlier_state
    tail = jnp.stack([keys, values], axis=0)
    arrived = from_behind(tail, "ctx", 1)
    past = jnp.transpose(past_kv.reshape(2, WINDOW, local_heads, HDIM), (0, 2, 1, 3))
    previous = jnp.where(lax.axis_index("ctx") == 0, past, arrived)
    all_keys = jnp.concatenate([previous[0], keys], axis=1)
    all_values = jnp.concatenate([previous[1], values], axis=1)
    block_rows = min(slab_rows, 512)
    block_count = slab_rows // block_rows
    scale = 1.0 / math.sqrt(HDIM)
    causal = jnp.arange(block_rows)[:, None] >= jnp.arange(block_rows)[None, :]
    offsets = jnp.arange(WINDOW + block_rows)[None, :] - jnp.arange(block_rows)[:, None]
    in_window = (offsets > 0) & (offsets <= WINDOW)

    def block_step(state, index):
        first = index * block_rows
        carried = jnp.einsum(
            "hsd,hde->hse", query.astype(jnp.float32), state, precision=lax.Precision.HIGHEST
        )
        inside = jnp.einsum("hsd,htd->hst", query, keys, preferred_element_type=jnp.float32)
        inside = jnp.where(causal[None], inside, 0.0).astype(jnp.bfloat16)
        linear = carried + jnp.einsum(
            "hst,hte->hse", inside, values, preferred_element_type=jnp.float32
        )
        scores = (
            jnp.einsum("hsd,htd->hst", query, all_keys, preferred_element_type=jnp.float32) * scale
        )
        scores = jnp.where(in_window[None], scores, -jnp.inf)
        top_score = jnp.max(scores, axis=-1, keepdims=True)
        expo = jnp.exp(scores - top_score)
        probs = (expo / jnp.sum(expo, axis=-1, keepdims=True)).astype(jnp.bfloat16)
        window_out = jnp.einsum(
            "hst,hte->hse", probs, all_values, preferred_element_type=jnp.float32
        )
        combined = (normalize(linear) + window_out).astype(jnp.bfloat16)
        new_state = state + jnp.einsum(
            "hsd,hse->hde", keys, values, preferred_element_type=jnp.float32
        )
        return (new_state, combined)

    _, outs = lax.scan(block_step, start_state, jnp.arange(block_count, dtype=jnp.int32))
    heads_out = jnp.transpose(outs, (0, 2, 1, 3)).reshape(slab_rows, inner_width)
    regrouped = lax.all_to_all(heads_out, "heads", split_axis=0, concat_axis=1, tiled=True)
    attn = jnp.dot(
        regrouped,
        lax.all_gather(w_out, "heads", axis=0, tiled=True),
        preferred_element_type=jnp.float32,
    )
    hidden_state = (tokens.astype(jnp.float32) + attn).astype(jnp.bfloat16)
    hidden_float = hidden_state.astype(jnp.float32)
    normed = normalize(hidden_float).astype(jnp.bfloat16)
    ctx_count = lax.axis_size("ctx")
    head_count = lax.axis_size("heads")
    exp_local = w_gate.shape[0]
    expert_count = exp_local * ctx_count * head_count
    top_count = expert_ids.shape[1]
    capacity = max(2, 2 * row_count * top_count // expert_count)
    devices = ctx_count * head_count
    if row_count * devices <= expert_count * capacity:
        return dense_experts(
            hidden_float, normed, w_gate, w_up, w_down, expert_ids, gate_weights, expert_count
        )
    picks = expert_ids.reshape(-1)
    onehot = (picks[:, None] == jnp.arange(expert_count, dtype=jnp.int32)[None, :]).astype(
        jnp.int32
    )
    earlier = jnp.cumsum(onehot, axis=0) - onehot
    slots = jnp.sum(onehot * earlier, axis=1)
    destination = picks * capacity + slots
    source_rows = jnp.arange(row_count * top_count, dtype=jnp.int32) // top_count
    outgoing = jnp.zeros((expert_count * capacity, model_width), jnp.bfloat16)
    outgoing = outgoing.at[destination].set(normed[source_rows])
    sendable = outgoing.reshape(expert_count, 1, capacity, model_width)
    arrived_rows = lax.all_to_all(
        sendable, ("ctx", "heads"), split_axis=0, concat_axis=1, tiled=True
    )
    e_count, n_count, c_count, d_count = arrived_rows.shape
    flat = arrived_rows.reshape(e_count, n_count * c_count, d_count)
    gate_act = jnp.einsum("erd,edf->erf", flat, w_gate, preferred_element_type=jnp.float32)
    up_act = jnp.einsum("erd,edf->erf", flat, w_up, preferred_element_type=jnp.float32)
    hid = (jax.nn.silu(gate_act) * up_act).astype(jnp.bfloat16)
    out_rows = jnp.einsum("erf,efd->erd", hid, w_down, preferred_element_type=jnp.float32)
    finished = out_rows.astype(jnp.bfloat16).reshape(e_count, n_count, c_count, d_count)
    returned = lax.all_to_all(finished, ("ctx", "heads"), split_axis=1, concat_axis=0, tiled=True)
    returned = returned.reshape(expert_count * capacity, model_width)
    picked = returned[destination].reshape(row_count, top_count, model_width).astype(jnp.float32)
    routed = jnp.sum(gate_weights[:, :, None] * picked, axis=1)
    return (hidden_float + routed).astype(jnp.bfloat16)


def solution(mesh):
    return jax.shard_map(
        on_device,
        mesh=mesh,
        in_specs=(
            P(("groups", "ctx", "heads"), None),
            P("heads", "groups", None),
            P(None, "groups", "heads"),
            P(None, None, "heads"),
            P("heads", None),
            P(("ctx", "heads"), None, None),
            P(("ctx", "heads"), None, None),
            P(("ctx", "heads"), None, None),
            P(("groups", "ctx", "heads"), None),
            P(("groups", "ctx", "heads"), None),
        ),
        out_specs=P(("groups", "ctx", "heads"), None),
        check_vma=False,
    )
```

profile of v0, /device:TPU:0, one launch (start us, length us, event | category | flops | bytes accessed | tf_op | source)
XLA Modules:
  0.0 328.5 jit_solution(8045174008604358506)
XLA Ops:
  6.5 0.7 all-gather.5.cloned.1.call-update
  7.3 0.7 all-gather.7.cloned.1.call-update
  8.0 2.6 copy.27
  10.6 46.7 %all-gather.5.cloned.1.call-done = bf16[512,2048]{1,0:T(8,128)(2,1)} async-done(((bf16[128,2048]{1,0:T(8,128)(2,1)}), bf16[512,2048]{1,0:T(8,128)(2,1)}) %all-gather.5.cloned.1.call-update) | async-done | bytes 2097168 | tf_op jit(solution)/shard_map/all_gather | solution.py:63
  57.3 3.1 convolution_convert_fusion
  60.4 0.2 convolution_convert_fusion.1
  60.6 0.7 fusion.38
  61.3 5.4 %all-gather = bf16[512,128]{1,0:T(8,128)(2,1)S(1)} all-gather(bf16[128,128]{1,0:T(8,128)(2,1)S(1)} %convolution_convert_fusion.1), channel_id=2, replica_groups=mesh['groups'=2,'ctx'=4,'heads'=4] {'ctx'}, dimensions={0}, use_global_device_ids=true | all-gather | bytes 163840 | tf_op jit(solution)/shard_map/all_gather | solution.py:13
  66.7 1.0 copy.35
  67.8 1.7 copy.34
  69.4 1.6 pad_maximum_fusion
  71.1 3.0 collective-permute-start
  74.0 2.0 fusion.26
  76.0 2.3 multiply_reduce_fusion.1
  78.3 1.1 bitcast_select_fusion
  79.4 1.5 fusion.39
  80.9 0.5 fusion.11
  81.5 0.6 fusion.15
  82.1 0.8 copy.33
  82.8 3.5 %all-to-all-start = ((bf16[4,128,128]{1,2,0:T(8,128)(2,1)}), bf16[4,128,128]{1,2,0:T(8,128)(2,1)S(1)}, u32[]{:S(2)}, u32[]{:S(2)}) async-start(bf16[4,128,128]{1,2,0:T(8,128)(2,1)} %copy.33), calls=%async_computation | async-start | bytes 262144 | tf_op jit(solution)/shard_map/all_to_all | solution.py:118
  86.3 0.0 all-gather.9.cloned.1.call-start
  86.3 19.8 %all-gather.7.cloned.1.call-done = bf16[512,2048]{1,0:T(8,128)(2,1)} async-done(((bf16[128,2048]{1,0:T(8,128)(2,1)}), bf16[512,2048]{1,0:T(8,128)(2,1)}) %all-gather.7.cloned.1.call-update) | async-done | bytes 2097168 | tf_op jit(solution)/shard_map/all_gather | solution.py:121
  106.2 2.2 multiply_reduce_fusion
  108.4 1.0 copy-done.1
  109.4 0.9 multiply_convert_fusion.2
  110.4 0.0 reduce-scatter.2.cloned.1.call-start
  110.5 33.1 %all_gather.22 = f32[2048,16]{0,1:T(8,128)S(1)} all-gather(f32[128,16]{0,1:T(8,128)S(1)} %select_reduce_fusion), channel_id=1, replica_groups=mesh['groups'=2,'ctx'=4,'heads'=4] {'ctx','heads'}, dimensions={0}, use_global_device_ids=true | all-gather | bytes 139264 | tf_op jit(solution)/shard_map/all_gather | solution.py:39
  143.6 41.7 %all-gather.9.cloned.1.call-done = bf16[2048,2048]{1,0:T(8,128)(2,1)} async-done(((bf16[128,2048]{1,0:T(8,128)(2,1)}), bf16[2048,2048]{1,0:T(8,128)(2,1)}) %all-gather.9.cloned.1.call-update) | async-done | bytes 8388624 | tf_op jit(solution)/shard_map/all_gather | solution.py:41
  185.3 11.7 %fusion.3 = f32[2048,768]{1,0:T(8,128)} fusion(bf16[2048,2048]{1,0:T(8,128)(2,1)} %all-gather.9.cloned.1.call-done, bf16[1,2048,768]{2,1,0:T(8,128)(2,1)} %param.17), kind=kOutput, calls=%fused_computation.5 | convolution fusion | flops 6442450944 | bytes 17825792 | tf_op jit(solution)/shard_map/dot_general | solution.py:44
  197.0 20.6 %multiply_convert_fusion = bf16[2048,2048]{1,0:T(8,128)(2,1)} fusion(f32[2048]{0:T(1024)S(1)} %bitcast.98, f32[2048,768]{1,0:T(8,128)} %fusion.3, bf16[2048,2048]{1,0:T(8,128)(2,1)} %all-gather.9.cloned.1.call-done, bf16[1,768,2048]{2,1,0:T(8,128)(2,1)S(1)} %copy-done, bf16[1,2048,768]{2,1,0:T(8,128)(2,1)} %param.18), kind=kOutput, calls=%fused_computation.1 | convolution fusion | flops 12902727680 | bytes 29368320 | tf_op jit(solution)/shard_map/dot_general | solution.py:47
  217.6 102.2 %reduce-scatter.2.cloned.1.call-done = bf16[128,2048]{1,0:T(8,128)(2,1)} async-done(((bf16[2048,2048]{1,0:T(8,128)(2,1)}), bf16[128,2048]{1,0:T(8,128)(2,1)}) %reduce-scatter.2.cloned.1.call-update) | async-done | bytes 524304 | tf_op jit(solution)/shard_map/reduce_scatter | solution.py:51
  319.7 2.3 add_convert_fusion
  (29 shorter events, 0.2 us)
Async XLA Ops:
  6.5 190.4 %copy-start = (bf16[1,768,2048]{2,1,0:T(8,128)(2,1)S(1)}, bf16[1,768,2048]{2,1,0:T(8,128)(2,1)}, u32[]{:S(2)}) copy-start(bf16[1,768,2048]{2,1,0:T(8,128)(2,1)} %param.19) | copy-start | bytes 9437188
  6.5 50.8 %all-gather.5.cloned.1.call-start = ((), (), s32[]{:S(2)}) async-start(), calls=%async_computation.2 | async-start | bytes 2621440 | tf_op jit(solution)/shard_map/all_gather | solution.py:63
  7.3 98.9 %all-gather.7.cloned.1.call-start = ((), (), s32[]{:S(2)}) async-start(), calls=%async_computation.3 | async-start | bytes 2621440 | tf_op jit(solution)/shard_map/all_gather | solution.py:121
  57.3 16.7 %copy-start.4 = (f32[1,128,128]{2,1,0:T(8,128)S(1)}, f32[1,128,128]{2,1,0:T(8,128)}, u32[]{:S(2)}) copy-start(f32[1,128,128]{2,1,0:T(8,128)} %param.13) | copy-start | bytes 196612
  60.4 6.3 %copy-start.3 = (bf16[512,384]{0,1:T(8,128)(2,1)}, bf16[512,384]{0,1:T(8,128)(2,1)S(1)}, u32[]{:S(2)}) copy-start(bf16[512,384]{0,1:T(8,128)(2,1)S(1)} %convolution_convert_fusion) | copy-start | bytes 1179652
  71.1 7.3 %collective-permute-start = (bf16[2,1,512,128]{3,2,1,0:T(8,128)(2,1)}, bf16[2,1,512,128]{3,2,1,0:T(8,128)(2,1)}, u32[]{:S(2)}, u32[]{:S(2)}) collective-permute-start(bf16[2,1,512,128]{3,2,1,0:T(8,128)(2,1)} %pad_maximum_fusion), channel_id=1, source_target_pairs={{0,4},{4,8},{8,12},{1,5},{5,9},{9,13},{2,6},{6,10},{10,14},{3,7},{... | collective-permute-start | bytes 786440 | tf_op jit(solution)/shard_map/ppermute | solution.py:25
  74.0 5.4 %copy-start.2 = (bf16[512,1,1,128]{3,0,2,1:T(8,128)(2,1)S(1)}, bf16[512,1,1,128]{3,0,2,1:T(8,128)(2,1)}, u32[]{:S(2)}) copy-start(bf16[512,1,1,128]{3,0,2,1:T(8,128)(2,1)} %copy.34) | copy-start | bytes 393220
  79.4 2.1 copy-start.7
  82.8 27.6 %copy-start.5 = (f32[128,8]{0,1:T(8,128)S(1)}, f32[128,8]{0,1:T(8,128)}, u32[]{:S(2)}) copy-start(f32[128,8]{0,1:T(8,128)} %param.21) | copy-start | bytes 12292
  82.8 27.6 %copy-start.6 = (s32[128,8]{0,1:T(8,128)S(1)}, s32[128,8]{0,1:T(8,128)}, u32[]{:S(2)}) copy-start(s32[128,8]{0,1:T(8,128)} %param.20) | copy-start | bytes 12292
  82.8 23.4 %all-to-all-start = ((bf16[4,128,128]{1,2,0:T(8,128)(2,1)}), bf16[4,128,128]{1,2,0:T(8,128)(2,1)S(1)}, u32[]{:S(2)}, u32[]{:S(2)}) async-start(bf16[4,128,128]{1,2,0:T(8,128)(2,1)} %copy.33), calls=%async_computation | async-start | bytes 262144 | tf_op jit(solution)/shard_map/all_to_all | solution.py:118
  86.3 99.0 %all-gather.9.cloned.1.call-start = ((), (), s32[]{:S(2)}) async-start(), calls=%async_computation.4 | async-start | bytes 8912896 | tf_op jit(solution)/shard_map/all_gather | solution.py:41
  108.4 1.0 copy-start.1
  110.4 209.4 %reduce-scatter.2.cloned.1.call-start = ((), (), s32[]{:S(2)}) async-start(), calls=%async_computation.5 | async-start | bytes 8912896 | tf_op jit(solution)/shard_map/reduce_scatter | solution.py:51
Sparse Core Ops, SparseCore 0:
  8.9 48.3 all-gather.4
  58.9 47.2 all-gather.6
  110.5 74.7 all-gather.8
  217.7 101.9 reduce-scatter.1
where the time goes:
time: 329 us
  waiting for transfers between devices  212 us (64%)
  matrix products  44.1 us (13%)
  blocking collectives  38.5 us (12%)
  between operations  13.3 us (4%)
  local copies, waits for them, and re-layouts  7.86 us (2%)
  starting transfers between devices  6.54 us (2%)
  other arithmetic  6.41 us (2%)
    reduce_scatter x1, waiting for transfers between devices, dense_experts(): lax.psum_scatter(total.astype(jnp.bfloat16), axes, scatter_dimension=0, t...  102 us
    all_gather x1, waiting for transfers between devices, on_device(): lax.all_gather(tokens, 'heads', axis=0, tiled=True)  46.7 us
    all_gather x1, waiting for transfers between devices, dense_experts(): rows = lax.all_gather(normed, axes, axis=0, tiled=True)  41.7 us
    all_gather x1, blocking collectives, dense_experts(): weights = lax.all_gather(table, axes, axis=0, tiled=True)  33.1 us
    dot_general x1, matrix products, dense_experts(): out_rows = jnp.dot(hid, w_down[e], preferred_element_type=jnp.float32)  20.6 us
    all_gather x1, waiting for transfers between devices, on_device(): lax.all_gather(w_out, 'heads', axis=0, tiled=True)  19.8 us
    dot_general x1, matrix products, dense_experts(): gate_act = jnp.dot(rows, w_gate[e], preferred_element_type=jnp.float32)  11.7 us
  transfers between devices with their start and end apart: 6, of which 4 were waited for; matrix products, arithmetic and copies ran while one was open for 6% of the time, Pallas kernels for 0%

commit v1 on v0

--- a/solution.py
+++ b/solution.py
@@ -1,3 +1,4 @@
+import functools
 import math
 import jax
 import jax.numpy as jnp
@@ -6,6 +7,22 @@
 
 HDIM = 128
 WINDOW = 512
+
+
+def figure_report(local_array, chip_axis):
+    dev_count = lax.axis_size(chip_axis)
+    store = [local_array]
+    for jj in range(1, dev_count):
+        ready = lax.ppermute(
+            store[jj - 1], chip_axis, [(it, (it - 1) % dev_count) for it in range(dev_count)]
+        )
+        store.append(ready)
+    shaped = jnp.concatenate(store, axis=0)
+    a_now = lax.axis_index(chip_axis)
+    return jnp.roll(shaped, a_now * local_array.shape[0], axis=0)
+
+
+_treat_arrays = functools.partial(figure_report, chip_axis="heads")
 
 
 def entering(x, axis, join, neutral):
@@ -116,11 +133,7 @@
     _, outs = lax.scan(block_step, start_state, jnp.arange(block_count, dtype=jnp.int32))
     heads_out = jnp.transpose(outs, (0, 2, 1, 3)).reshape(slab_rows, inner_width)
     regrouped = lax.all_to_all(heads_out, "heads", split_axis=0, concat_axis=1, tiled=True)
-    attn = jnp.dot(
-        regrouped,
-        lax.all_gather(w_out, "heads", axis=0, tiled=True),
-        preferred_element_type=jnp.float32,
-    )
+    attn = jnp.dot(regrouped, _treat_arrays(w_out), preferred_element_type=jnp.float32)
     hidden_state = (tokens.astype(jnp.float32) + attn).astype(jnp.bfloat16)
     hidden_float = hidden_state.astype(jnp.float32)
     normed = normalize(hidden_float).astype(jnp.bfloat16)

time: 329 us -> 347 us (1.055)
  local copies, waits for them, and re-layouts: 7.86 us -> 21.8 us
  starting transfers between devices: 6.54 us -> 17.9 us
  waiting for transfers between devices: 212 us -> 205 us
    ppermute x0 -> x3, waiting for transfers between devices: none -> 54.6 us  [figure_report(): lax.ppermute(store[jj - 1], chip_axis, [(it, (it - 1) % dev_count) for it...]
    all_gather x1, waiting for transfers between devices: 46.7 us -> 0.01 us  [on_device(): lax.all_gather(tokens, 'heads', axis=0, tiled=True)]
    all_gather x1 -> x0, waiting for transfers between devices: 19.8 us -> none  [on_device(): lax.all_gather(w_out, 'heads', axis=0, tiled=True)]
    unnamed x19 -> x28, local copies, waits for them, and re-layouts: 6.34 us -> 18.5 us
    ppermute x0 -> x3, starting transfers between devices: none -> 9.31 us  [figure_report(): lax.ppermute(store[jj - 1], chip_axis, [(it, (it - 1) % dev_count) for it...]
    all_to_all x1, waiting for transfers between devices: 0.01 us -> 4.62 us  [on_device(): lax.all_to_all(heads_out, 'heads', split_axis=0, concat_axis=1, tiled=True)]
  transfers between devices with their start and end apart: 6 -> 8, of which waited for: 4 -> 6; matrix products, arithmetic and copies ran while one was open for 6% -> 6% of each run, Pallas kernels for 0% -> 0%
where the time goes in v1:
time: 347 us; the launch traced here: 346 us
  waiting for transfers between devices  205 us (59%)
  matrix products  44.1 us (13%)
  blocking collectives  38.1 us (11%)
  local copies, waits for them, and re-layouts  21.8 us (6%)
  starting transfers between devices  17.9 us (5%)
  between operations  13.3 us (4%)
  other arithmetic  6.45 us (2%)
    reduce_scatter x1, waiting for transfers between devices, dense_experts(): lax.psum_scatter(total.astype(jnp.bfloat16), axes, scatter_dimension=0, t...  102 us
    ppermute x3, waiting for transfers between devices, figure_report(): lax.ppermute(store[jj - 1], chip_axis, [(it, (it - 1) % dev_count) for it...  54.6 us
    all_gather x1, waiting for transfers between devices, dense_experts(): rows = lax.all_gather(normed, axes, axis=0, tiled=True)  42.6 us
    all_gather x1, blocking collectives, dense_experts(): weights = lax.all_gather(table, axes, axis=0, tiled=True)  32.7 us
    dot_general x1, matrix products, dense_experts(): out_rows = jnp.dot(hid, w_down[e], preferred_element_type=jnp.float32)  20.6 us
    unnamed x28, local copies, waits for them, and re-layouts  18.5 us
    dot_general x1, matrix products, dense_experts(): gate_act = jnp.dot(rows, w_gate[e], preferred_element_type=jnp.float32)  11.7 us
    ppermute x3, starting transfers between devices, figure_report(): lax.ppermute(store[jj - 1], chip_axis, [(it, (it - 1) % dev_count) for it...  9.31 us
  transfers between devices with their start and end apart: 8, of which 6 were waited for; matrix products, arithmetic and copies ran while one was open for 6% of the time, Pallas kernels for 0%

profile of v1, /device:TPU:0, one launch (start us, length us, event | category | flops | bytes accessed | tf_op | source)
XLA Modules:
  0.0 346.3 jit_solution(7733743988309428497)
XLA Ops:
  7.3 5.1 %collective-permute-start.1 = (bf16[128,2048]{1,0:T(8,128)(2,1)}, bf16[128,2048]{1,0:T(8,128)(2,1)S(1)}, u32[]{:S(2)}, u32[]{:S(2)}) collective-permute-start(bf16[128,2048]{1,0:T(8,128)(2,1)} %param.16), channel_id=1, source_target_pairs={{0,3},{1,0},{2,1},{3,2},{4,7},{5,4},{6,5},{7,6},{8,11},{9,8},{10,9... | collective-permute-start | bytes 1572872 | tf_op jit(solution)/shard_map/ppermute | solution.py:16
  12.4 16.6 %collective-permute-done.1 = bf16[128,2048]{1,0:T(8,128)(2,1)S(1)} collective-permute-done((bf16[128,2048]{1,0:T(8,128)(2,1)}, bf16[128,2048]{1,0:T(8,128)(2,1)S(1)}, u32[]{:S(2)}, u32[]{:S(2)}) %collective-permute-start.1) | collective-permute-done | bytes 524320 | tf_op jit(solution)/shard_map/ppermute | solution.py:16
  29.7 4.2 %collective-permute-start.2 = (bf16[128,2048]{1,0:T(8,128)(2,1)S(1)}, bf16[128,2048]{1,0:T(8,128)(2,1)}, u32[]{:S(2)}, u32[]{:S(2)}) collective-permute-start(bf16[128,2048]{1,0:T(8,128)(2,1)S(1)} %collective-permute-done.1), channel_id=1, source_target_pairs={{0,3},{1,0},{2,1},{3,2},{4,7},{5,4},{6,5},{7,6},{8,11},{9,8},{10,9... | collective-permute-start | bytes 1572872 | tf_op jit(solution)/shard_map/ppermute | solution.py:16
  33.9 34.0 %collective-permute-done.2 = bf16[128,2048]{1,0:T(8,128)(2,1)} collective-permute-done((bf16[128,2048]{1,0:T(8,128)(2,1)S(1)}, bf16[128,2048]{1,0:T(8,128)(2,1)}, u32[]{:S(2)}, u32[]{:S(2)}) %collective-permute-start.2) | collective-permute-done | bytes 524320 | tf_op jit(solution)/shard_map/ppermute | solution.py:16
  67.9 1.9 constant_dynamic-update-slice_fusion.7
  69.8 2.6 copy.27
  72.4 1.9 constant_dynamic-update-slice_fusion.6
  74.4 1.9 constant_dynamic-update-slice_fusion.5
  76.3 4.0 %collective-permute-done.3 = bf16[128,2048]{1,0:T(8,128)(2,1)} collective-permute-done((bf16[128,2048]{1,0:T(8,128)(2,1)}, bf16[128,2048]{1,0:T(8,128)(2,1)}, u32[]{:S(2)}, u32[]{:S(2)}) %collective-permute-start.3) | collective-permute-done | bytes 524320 | tf_op jit(solution)/shard_map/ppermute | solution.py:16
  80.3 1.9 constant_dynamic-update-slice_fusion.4
  82.2 1.9 constant_dynamic-update-slice_fusion.3
  84.9 1.9 constant_dynamic-update-slice_fusion.1
  86.8 3.1 convolution_convert_fusion
  90.8 5.4 %all-gather = bf16[512,128]{1,0:T(8,128)(2,1)S(1)} all-gather(bf16[128,128]{1,0:T(8,128)(2,1)S(1)} %convolution_convert_fusion.1), channel_id=2, replica_groups=mesh['groups'=2,'ctx'=4,'heads'=4] {'ctx'}, dimensions={0}, use_global_device_ids=true | all-gather | bytes 163840 | tf_op jit(solution)/shard_map/all_gather | solution.py:30
  96.2 1.0 copy.35
  98.0 1.6 pad_maximum_fusion
  99.6 3.0 collective-permute-start
  102.6 1.9 fusion.27
  104.6 2.3 multiply_reduce_fusion.1
  106.9 1.1 bitcast_select_fusion
  108.0 1.5 fusion.41
  111.5 5.5 %all-to-all-start = ((bf16[4,128,128]{1,2,0:T(8,128)(2,1)}), bf16[4,128,128]{1,2,0:T(8,128)(2,1)S(1)}, u32[]{:S(2)}, u32[]{:S(2)}) async-start(bf16[4,128,128]{1,2,0:T(8,128)(2,1)} %copy.33), calls=%async_computation | async-start | bytes 262144 | tf_op jit(solution)/shard_map/all_to_all | solution.py:135
  117.0 1.9 constant_dynamic-update-slice_fusion
  118.9 4.6 %all-to-all-done = bf16[4,128,128]{1,2,0:T(8,128)(2,1)S(1)} async-done(((bf16[4,128,128]{1,2,0:T(8,128)(2,1)}), bf16[4,128,128]{1,2,0:T(8,128)(2,1)S(1)}, u32[]{:S(2)}, u32[]{:S(2)}) %all-to-all-start) | async-done | bytes 131104 | tf_op jit(solution)/shard_map/all_to_all | solution.py:135
  123.5 2.2 multiply_reduce_fusion
  125.8 1.0 copy-done.1
  127.8 32.7 %all_gather.18 = f32[2048,16]{0,1:T(8,128)S(1)} all-gather(f32[128,16]{0,1:T(8,128)S(1)} %select_reduce_fusion), channel_id=1, replica_groups=mesh['groups'=2,'ctx'=4,'heads'=4] {'ctx','heads'}, dimensions={0}, use_global_device_ids=true | all-gather | bytes 139264 | tf_op jit(solution)/shard_map/all_gather | solution.py:56
  160.4 42.6 %all-gather.6.cloned.1.call-done = bf16[2048,2048]{1,0:T(8,128)(2,1)} async-done(((bf16[128,2048]{1,0:T(8,128)(2,1)}), bf16[2048,2048]{1,0:T(8,128)(2,1)}) %all-gather.6.cloned.1.call-update) | async-done | bytes 8388624 | tf_op jit(solution)/shard_map/all_gather | solution.py:58
  203.0 11.7 %fusion.3 = f32[2048,768]{1,0:T(8,128)} fusion(bf16[2048,2048]{1,0:T(8,128)(2,1)} %all-gather.6.cloned.1.call-done, bf16[1,2048,768]{2,1,0:T(8,128)(2,1)} %param.17), kind=kOutput, calls=%fused_computation.5 | convolution fusion | flops 6442450944 | bytes 17825792 | tf_op jit(solution)/shard_map/dot_general | solution.py:61
  214.7 20.6 %multiply_convert_fusion = bf16[2048,2048]{1,0:T(8,128)(2,1)} fusion(f32[2048]{0:T(1024)S(1)} %bitcast.97, f32[2048,768]{1,0:T(8,128)} %fusion.3, bf16[2048,2048]{1,0:T(8,128)(2,1)} %all-gather.6.cloned.1.call-done, bf16[1,768,2048]{2,1,0:T(8,128)(2,1)S(1)} %copy-done, bf16[1,2048,768]{2,1,0:T(8,128)(2,1)} %param.18), kind=kOutput, calls=%fused_computation.1 | convolution fusion | flops 12902727680 | bytes 29368320 | tf_op jit(solution)/shard_map/dot_general | solution.py:64
  235.3 102.2 %reduce-scatter.2.cloned.1.call-done = bf16[128,2048]{1,0:T(8,128)(2,1)} async-done(((bf16[2048,2048]{1,0:T(8,128)(2,1)}), bf16[128,2048]{1,0:T(8,128)(2,1)}) %reduce-scatter.2.cloned.1.call-update) | async-done | bytes 524304 | tf_op jit(solution)/shard_map/reduce_scatter | solution.py:68
  337.5 2.3 add_convert_fusion
  (42 shorter events, 6.9 us)
Async XLA Ops:
  6.5 208.2 %copy-start = (bf16[1,768,2048]{2,1,0:T(8,128)(2,1)S(1)}, bf16[1,768,2048]{2,1,0:T(8,128)(2,1)}, u32[]{:S(2)}) copy-start(bf16[1,768,2048]{2,1,0:T(8,128)(2,1)} %param.19) | copy-start | bytes 9437188
  6.5 80.3 %all-gather.4.cloned.1.call-start = ((), (), s32[]{:S(2)}) async-start(), calls=%async_computation.2 | async-start | bytes 2621440 | tf_op jit(solution)/shard_map/all_gather | solution.py:80
  7.3 21.7 %collective-permute-start.1 = (bf16[128,2048]{1,0:T(8,128)(2,1)}, bf16[128,2048]{1,0:T(8,128)(2,1)S(1)}, u32[]{:S(2)}, u32[]{:S(2)}) collective-permute-start(bf16[128,2048]{1,0:T(8,128)(2,1)} %param.16), channel_id=1, source_target_pairs={{0,3},{1,0},{2,1},{3,2},{4,7},{5,4},{6,5},{7,6},{8,11},{9,8},{10,9... | collective-permute-start | bytes 1572872 | tf_op jit(solution)/shard_map/ppermute | solution.py:16
  28.9 0.8 copy-start.2
  29.7 38.2 %collective-permute-start.2 = (bf16[128,2048]{1,0:T(8,128)(2,1)S(1)}, bf16[128,2048]{1,0:T(8,128)(2,1)}, u32[]{:S(2)}, u32[]{:S(2)}) collective-permute-start(bf16[128,2048]{1,0:T(8,128)(2,1)S(1)} %collective-permute-done.1), channel_id=1, source_target_pairs={{0,3},{1,0},{2,1},{3,2},{4,7},{5,4},{6,5},{7,6},{8,11},{9,8},{10,9... | collective-permute-start | bytes 1572872 | tf_op jit(solution)/shard_map/ppermute | solution.py:16
  67.9 12.4 %collective-permute-start.3 = (bf16[128,2048]{1,0:T(8,128)(2,1)}, bf16[128,2048]{1,0:T(8,128)(2,1)}, u32[]{:S(2)}, u32[]{:S(2)}) collective-permute-start(bf16[128,2048]{1,0:T(8,128)(2,1)} %collective-permute-done.2), channel_id=1, source_target_pairs={{0,3},{1,0},{2,1},{3,2},{4,7},{5,4},{6,5},{7,6},{8,11},{9,8},{10,9... | collective-permute-start | bytes 1572872 | tf_op jit(solution)/shard_map/ppermute | solution.py:16
  72.4 11.6 %copy-start.3 = (bf16[128,2048]{1,0:T(8,128)(2,1)S(1)}, bf16[128,2048]{1,0:T(8,128)(2,1)}, u32[]{:S(2)}) copy-start(bf16[128,2048]{1,0:T(8,128)(2,1)} %copy-done.2) | copy-start | bytes 1572868
  86.8 15.8 %copy-start.5 = (f32[1,128,128]{2,1,0:T(8,128)S(1)}, f32[1,128,128]{2,1,0:T(8,128)}, u32[]{:S(2)}) copy-start(f32[1,128,128]{2,1,0:T(8,128)} %param.13) | copy-start | bytes 196612
  89.9 6.3 %copy-start.4 = (bf16[512,384]{0,1:T(8,128)(2,1)}, bf16[512,384]{0,1:T(8,128)(2,1)S(1)}, u32[]{:S(2)}) copy-start(bf16[512,384]{0,1:T(8,128)(2,1)S(1)} %convolution_convert_fusion) | copy-start | bytes 1179652
  99.6 7.3 %collective-permute-start = (bf16[2,1,512,128]{3,2,1,0:T(8,128)(2,1)}, bf16[2,1,512,128]{3,2,1,0:T(8,128)(2,1)}, u32[]{:S(2)}, u32[]{:S(2)}) collective-permute-start(bf16[2,1,512,128]{3,2,1,0:T(8,128)(2,1)} %pad_maximum_fusion), channel_id=1, source_target_pairs={{0,4},{4,8},{8,12},{1,5},{5,9},{9,13},{2,6},{6,10},{10,14},{3,7},{... | collective-permute-start | bytes 786440 | tf_op jit(solution)/shard_map/ppermute | solution.py:42
  106.9 3.2 copy-start.8
  110.7 17.1 %copy-start.6 = (f32[128,8]{0,1:T(8,128)S(1)}, f32[128,8]{0,1:T(8,128)}, u32[]{:S(2)}) copy-start(f32[128,8]{0,1:T(8,128)} %param.21) | copy-start | bytes 12292
  110.7 17.1 %copy-start.7 = (s32[128,8]{0,1:T(8,128)S(1)}, s32[128,8]{0,1:T(8,128)}, u32[]{:S(2)}) copy-start(s32[128,8]{0,1:T(8,128)} %param.20) | copy-start | bytes 12292
  111.5 12.1 %all-to-all-start = ((bf16[4,128,128]{1,2,0:T(8,128)(2,1)}), bf16[4,128,128]{1,2,0:T(8,128)(2,1)S(1)}, u32[]{:S(2)}, u32[]{:S(2)}) async-start(bf16[4,128,128]{1,2,0:T(8,128)(2,1)} %copy.33), calls=%async_computation | async-start | bytes 262144 | tf_op jit(solution)/shard_map/all_to_all | solution.py:135
  117.0 86.0 %all-gather.6.cloned.1.call-start = ((), (), s32[]{:S(2)}) async-start(), calls=%async_computation.3 | async-start | bytes 8912896 | tf_op jit(solution)/shard_map/all_gather | solution.py:58
  125.7 1.0 copy-start.1
  127.7 209.8 %reduce-scatter.2.cloned.1.call-start = ((), (), s32[]{:S(2)}) async-start(), calls=%async_computation.4 | async-start | bytes 8912896 | tf_op jit(solution)/shard_map/reduce_scatter | solution.py:68
Sparse Core Ops, SparseCore 0:
  8.9 62.7 all-gather.3
  127.8 75.1 all-gather.5
  235.4 102.0 reduce-scatter.1
